TPU v7x, 256 devices: a whole 4x4x8 slice. The times are simulated.
256 devices in a mesh: seq: 32 (over y, x, z_hi), head: 8 (over z_lo, core).
Axes of the slice: x: 4, y: 4, z: 8 (z_hi: 2, z_lo: 4; z = z_hi * 4 + z_lo), core: 2. Of those that a mesh axis runs over, the one named last changes fastest.
Arguments:
- queries: bfloat16 [16384, 4096], P(('seq', 'head')), may hold values from -72 to 72
- keys: bfloat16 [16384, 2048], P(('seq', 'head')), may hold values from -6 to 6
- values: bfloat16 [16384, 2048], P(('seq', 'head')), may hold values from -6 to 6
- prefix_keys: bfloat16 [4096, 2048], P(None, 'head'), may hold values from -10 to 10
- prefix_values: bfloat16 [4096, 2048], P(None, 'head'), may hold values from -6 to 6
- span_start: int32 [1], replicated, may hold values from 0 to 4095
Outputs:
- attended: bfloat16 [16384, 4096], P(('seq', 'head'))
All inputs are finite; a program needn't handle non-finite values.
Results may differ from a plain program's by a relative error of at most 0.003.
Values may be sent and summed in bfloat16 or wider, within the bound.
A program may use at most 128 MiB of HBM per device.

v0:
```python
import jax
import jax.numpy as jnp
from jax import lax
from jax.sharding import PartitionSpec as P

HEAD_DIM = 128
QH = 32
KVH = 16
QSCALE = 144
WINDOW = 4096


def shifted(shard, axis, by):
    size = lax.axis_size(axis)
    pairs = [(i, i + by) for i in range(size) if 0 <= i + by < size]
    return lax.ppermute(shard, axis, pairs)


def shortened(shard):
    return jax.tree.map(lambda a: a.astype(jnp.bfloat16) if a.dtype == jnp.float32 else a, shard)


def attend_block(query_rows, key_rows, value_rows, query_first, key_first, start_value):
    block_rows = query_rows.shape[0]
    key_count = key_rows.shape[0]
    grouping = QH // KVH
    scaling = QSCALE ** (-0.5)
    local_groups = key_rows.shape[1] // HEAD_DIM
    query_pos = query_first + jnp.arange(block_rows, dtype=jnp.int32)
    key_pos = key_first + jnp.arange(key_count, dtype=jnp.int32)
    distance = query_pos[:, None] - key_pos[None, :]
    allowed = (distance >= 0) & (distance < WINDOW) & (start_value + key_pos >= 0)[None, :]
    outputs = []
    for key_group in range(local_groups):
        lower = key_group * grouping * HEAD_DIM
        query_head = query_rows[:, lower : lower + grouping * HEAD_DIM].reshape(
            block_rows, grouping, HEAD_DIM
        )
        key_head = key_rows[:, key_group * HEAD_DIM : (key_group + 1) * HEAD_DIM]
        value_head = value_rows[:, key_group * HEAD_DIM : (key_group + 1) * HEAD_DIM]
        scores = (
            jnp.einsum("qgd,kd->gqk", query_head, key_head, preferred_element_type=jnp.float32)
            * scaling
        )
        scores = jnp.where(allowed[None], scores, -jnp.inf)
        peak_score = jnp.max(scores, axis=2, keepdims=True)
        unnormed = jnp.exp(scores - peak_score)
        totals = jnp.sum(unnormed, axis=2)
        weights = unnormed.astype(jnp.bfloat16)
        mixture = jnp.einsum("gqk,kd->qgd", weights, value_head, preferred_element_type=jnp.float32)
        outputs.append(
            (mixture / jnp.transpose(totals)[:, :, None]).reshape(block_rows, grouping * HEAD_DIM)
        )
    return jnp.concatenate(outputs, axis=1).astype(jnp.bfloat16)


def shards(queries, keys, values, prefix_keys, prefix_values, span_start):
    query_local, key_local, value_local = (
        lax.all_to_all(queries, "head", split_axis=1, concat_axis=0, tiled=True),
        lax.all_to_all(keys, "head", split_axis=1, concat_axis=0, tiled=True),
        lax.all_to_all(values, "head", split_axis=1, concat_axis=0, tiled=True),
    )
    seq_rows = query_local.shape[0]
    shards_back = WINDOW // seq_rows
    seq_index = lax.axis_index("seq")

    def relay(step, carried):
        moving_keys, moving_values, window_keys, window_values = carried
        moving_keys, moving_values = shifted((moving_keys, moving_values), "seq", 1)
        offset = (shards_back - 1 - step) * seq_rows
        window_keys = lax.dynamic_update_slice_in_dim(window_keys, moving_keys, offset, 0)
        window_values = lax.dynamic_update_slice_in_dim(window_values, moving_values, offset, 0)
        return (moving_keys, moving_values, window_keys, window_values)

    empty = jnp.zeros((WINDOW, key_local.shape[1]), jnp.bfloat16)
    carried = lax.fori_loop(0, shards_back, relay, (key_local, value_local, empty, empty))
    window_keys = carried[2]
    window_values = carried[3]
    first_row = jnp.minimum(seq_index * seq_rows, WINDOW)
    padded_keys = jnp.concatenate([prefix_keys, jnp.zeros_like(prefix_keys)], axis=0)
    padded_values = jnp.concatenate([prefix_values, jnp.zeros_like(prefix_values)], axis=0)
    window_keys = window_keys + lax.dynamic_slice_in_dim(padded_keys, first_row, WINDOW, 0)
    window_values = window_values + lax.dynamic_slice_in_dim(padded_values, first_row, WINDOW, 0)
    all_keys = jnp.concatenate([window_keys, key_local], axis=0)
    all_values = jnp.concatenate([window_values, value_local], axis=0)
    block_rows = min(512, seq_rows)
    block_count = seq_rows // block_rows
    start_value = span_start[0]
    key_base = (seq_index - shards_back) * seq_rows
    query_base = seq_index * seq_rows

    def one_block(block_index):
        first = block_index * block_rows
        return attend_block(
            query_local, all_keys, all_values, query_base + first, key_base + first, start_value
        )

    blocks = lax.map(one_block, jnp.arange(block_count, dtype=jnp.int32))
    attended = blocks.reshape(seq_rows, query_local.shape[1])
    return lax.all_to_all(
        shortened(attended), "head", split_axis=0, concat_axis=1, tiled=True
    ).astype(attended.dtype)


def solution(mesh):
    placed = (
        P(("seq", "head"), None),
        P(("seq", "head"), None),
        P(("seq", "head"), None),
        P(None, "head"),
        P(None, "head"),
        P(),
    )
    return jax.shard_map(
        shards, mesh=mesh, in_specs=placed, out_specs=P(("seq", "head"), None), check_vma=False
    )
```

profile of v0, /device:TPU:16, one launch (start us, length us, event | category | flops | bytes accessed | tf_op | source)
XLA Modules:
  0.0 381.9 jit_solution(13669239722404619152)
XLA Ops:
  1.7 5.9 %all-to-all-start.1 = ((bf16[64,8,256]{2,0,1:T(8,128)(2,1)}), bf16[64,8,256]{2,0,1:T(8,128)(2,1)}, u32[]{:S(2)}, u32[]{:S(2)}) async-start(bf16[64,8,256]{2,0,1:T(8,128)(2,1)} %bitcast.95), calls=%async_computation.1 | async-start | bytes 524288 | tf_op jit(solution)/shard_map/all_to_all | solution.py:61
  10.0 7.5 %all-to-all-done.1 = bf16[64,8,256]{2,0,1:T(8,128)(2,1)} async-done(((bf16[64,8,256]{2,0,1:T(8,128)(2,1)}), bf16[64,8,256]{2,0,1:T(8,128)(2,1)}, u32[]{:S(2)}, u32[]{:S(2)}) %all-to-all-start.1) | async-done | bytes 262176 | tf_op jit(solution)/shard_map/all_to_all | solution.py:61
  25.6 4.1 %copy.44 = bf16[4096,256]{0,1:T(8,128)(2,1)} copy(bf16[4096,256]{1,0:T(8,128)(2,1)} %param.12) | data formatting | bytes 4194304 | tf_op args[4]
  31.5 5.0 %all-to-all-start.2 = ((bf16[64,8,512]{2,0,1:T(8,128)(2,1)}), bf16[64,8,512]{2,0,1:T(8,128)(2,1)}, u32[]{:S(2)}, u32[]{:S(2)}) async-start(bf16[64,8,512]{2,0,1:T(8,128)(2,1)} %bitcast.94), calls=%async_computation.2 | async-start | bytes 1048576 | tf_op jit(solution)/shard_map/all_to_all | solution.py:59
  40.3 204.3 %while.6 = (s32[]{:T(128)}, bf16[512,256]{1,0:T(8,128)(2,1)}, bf16[512,256]{1,0:T(8,128)(2,1)}, bf16[4096,256]{1,0:T(8,128)(2,1)}, bf16[4096,256]{0,1:T(8,128)(2...) while((s32[]{:T(128)}, bf16[512,256]{1,0:T(8,128)(2,1)}, bf16[512,256]{1,0:T(8,128)(2,1)}, ...), condition=%wide.region_1.0_spmd, body=%wide.region_0.0_spmd.sunk | while | flops 7 | bytes 4718839 | solution.py:76
  40.3 7.1 %collective-permute-start.1 = (bf16[512,256]{1,0:T(8,128)(2,1)}, bf16[512,256]{1,0:T(8,128)(2,1)S(1)}, u32[]{:S(2)}, u32[]{:S(2)}) collective-permute-start(bf16[512,256]{1,0:T(8,128)(2,1)} %get-tuple-element.191), channel_id=1, source_target_pairs={{0,8},{8,16},{16,24},{24,32},{32,40},{40,48},{48,56},{56,64},{64,7... | collective-permute-start | bytes 786440 | tf_op jit(solution)/shard_map/while/body/eval_jaxpr/ppermute | solution.py:16
  51.0 10.3 %collective-permute-done.1 = bf16[512,256]{1,0:T(8,128)(2,1)S(1)} collective-permute-done((bf16[512,256]{1,0:T(8,128)(2,1)}, bf16[512,256]{1,0:T(8,128)(2,1)S(1)}, u32[]{:S(2)}, u32[]{:S(2)}) %collective-permute-start.1) | collective-permute-done | bytes 262176 | tf_op jit(solution)/shard_map/while/body/eval_jaxpr/ppermute | solution.py:16
  62.8 6.7 %collective-permute-done = bf16[512,256]{1,0:T(8,128)(2,1)S(1)} collective-permute-done((bf16[512,256]{1,0:T(8,128)(2,1)}, bf16[512,256]{1,0:T(8,128)(2,1)S(1)}, u32[]{:S(2)}, u32[]{:S(2)}) %collective-permute-start) | collective-permute-done | bytes 262176 | tf_op jit(solution)/shard_map/while/body/eval_jaxpr/ppermute | solution.py:16
  73.6 5.9 %collective-permute-start = (bf16[512,256]{1,0:T(8,128)(2,1)}, bf16[512,256]{1,0:T(8,128)(2,1)S(1)}, u32[]{:S(2)}, u32[]{:S(2)}) collective-permute-start(bf16[512,256]{1,0:T(8,128)(2,1)} %get-tuple-element.190), channel_id=1, source_target_pairs={{0,8},{8,16},{16,24},{24,32},{32,40},{40,48},{48,56},{56,64},{64,7... | collective-permute-start | bytes 786440 | tf_op jit(solution)/shard_map/while/body/eval_jaxpr/ppermute | solution.py:16
  79.6 9.6 %collective-permute-done.1 = bf16[512,256]{1,0:T(8,128)(2,1)S(1)} collective-permute-done((bf16[512,256]{1,0:T(8,128)(2,1)}, bf16[512,256]{1,0:T(8,128)(2,1)S(1)}, u32[]{:S(2)}, u32[]{:S(2)}) %collective-permute-start.1) | collective-permute-done | bytes 262176 | tf_op jit(solution)/shard_map/while/body/eval_jaxpr/ppermute | solution.py:16
  97.4 4.3 %collective-permute-start = (bf16[512,256]{1,0:T(8,128)(2,1)}, bf16[512,256]{1,0:T(8,128)(2,1)S(1)}, u32[]{:S(2)}, u32[]{:S(2)}) collective-permute-start(bf16[512,256]{1,0:T(8,128)(2,1)} %get-tuple-element.190), channel_id=1, source_target_pairs={{0,8},{8,16},{16,24},{24,32},{32,40},{40,48},{48,56},{56,64},{64,7... | collective-permute-start | bytes 786440 | tf_op jit(solution)/shard_map/while/body/eval_jaxpr/ppermute | solution.py:16
  101.7 12.0 %collective-permute-done.1 = bf16[512,256]{1,0:T(8,128)(2,1)S(1)} collective-permute-done((bf16[512,256]{1,0:T(8,128)(2,1)}, bf16[512,256]{1,0:T(8,128)(2,1)S(1)}, u32[]{:S(2)}, u32[]{:S(2)}) %collective-permute-start.1) | collective-permute-done | bytes 262176 | tf_op jit(solution)/shard_map/while/body/eval_jaxpr/ppermute | solution.py:16
  120.9 4.8 %collective-permute-start = (bf16[512,256]{1,0:T(8,128)(2,1)}, bf16[512,256]{1,0:T(8,128)(2,1)S(1)}, u32[]{:S(2)}, u32[]{:S(2)}) collective-permute-start(bf16[512,256]{1,0:T(8,128)(2,1)} %get-tuple-element.190), channel_id=1, source_target_pairs={{0,8},{8,16},{16,24},{24,32},{32,40},{40,48},{48,56},{56,64},{64,7... | collective-permute-start | bytes 786440 | tf_op jit(solution)/shard_map/while/body/eval_jaxpr/ppermute | solution.py:16
  125.8 12.2 %collective-permute-done.1 = bf16[512,256]{1,0:T(8,128)(2,1)S(1)} collective-permute-done((bf16[512,256]{1,0:T(8,128)(2,1)}, bf16[512,256]{1,0:T(8,128)(2,1)S(1)}, u32[]{:S(2)}, u32[]{:S(2)}) %collective-permute-start.1) | collective-permute-done | bytes 262176 | tf_op jit(solution)/shard_map/while/body/eval_jaxpr/ppermute | solution.py:16
  139.6 4.0 %collective-permute-done = bf16[512,256]{1,0:T(8,128)(2,1)S(1)} collective-permute-done((bf16[512,256]{1,0:T(8,128)(2,1)}, bf16[512,256]{1,0:T(8,128)(2,1)S(1)}, u32[]{:S(2)}, u32[]{:S(2)}) %collective-permute-start) | collective-permute-done | bytes 262176 | tf_op jit(solution)/shard_map/while/body/eval_jaxpr/ppermute | solution.py:16
  147.0 4.5 %collective-permute-start = (bf16[512,256]{1,0:T(8,128)(2,1)}, bf16[512,256]{1,0:T(8,128)(2,1)S(1)}, u32[]{:S(2)}, u32[]{:S(2)}) collective-permute-start(bf16[512,256]{1,0:T(8,128)(2,1)} %get-tuple-element.190), channel_id=1, source_target_pairs={{0,8},{8,16},{16,24},{24,32},{32,40},{40,48},{48,56},{56,64},{64,7... | collective-permute-start | bytes 786440 | tf_op jit(solution)/shard_map/while/body/eval_jaxpr/ppermute | solution.py:16
  151.5 11.7 %collective-permute-done.1 = bf16[512,256]{1,0:T(8,128)(2,1)S(1)} collective-permute-done((bf16[512,256]{1,0:T(8,128)(2,1)}, bf16[512,256]{1,0:T(8,128)(2,1)S(1)}, u32[]{:S(2)}, u32[]{:S(2)}) %collective-permute-start.1) | collective-permute-done | bytes 262176 | tf_op jit(solution)/shard_map/while/body/eval_jaxpr/ppermute | solution.py:16
  171.4 4.1 %collective-permute-start = (bf16[512,256]{1,0:T(8,128)(2,1)}, bf16[512,256]{1,0:T(8,128)(2,1)S(1)}, u32[]{:S(2)}, u32[]{:S(2)}) collective-permute-start(bf16[512,256]{1,0:T(8,128)(2,1)} %get-tuple-element.190), channel_id=1, source_target_pairs={{0,8},{8,16},{16,24},{24,32},{32,40},{40,48},{48,56},{56,64},{64,7... | collective-permute-start | bytes 786440 | tf_op jit(solution)/shard_map/while/body/eval_jaxpr/ppermute | solution.py:16
  175.5 12.2 %collective-permute-done.1 = bf16[512,256]{1,0:T(8,128)(2,1)S(1)} collective-permute-done((bf16[512,256]{1,0:T(8,128)(2,1)}, bf16[512,256]{1,0:T(8,128)(2,1)S(1)}, u32[]{:S(2)}, u32[]{:S(2)}) %collective-permute-start.1) | collective-permute-done | bytes 262176 | tf_op jit(solution)/shard_map/while/body/eval_jaxpr/ppermute | solution.py:16
  189.4 4.0 %collective-permute-done = bf16[512,256]{1,0:T(8,128)(2,1)S(1)} collective-permute-done((bf16[512,256]{1,0:T(8,128)(2,1)}, bf16[512,256]{1,0:T(8,128)(2,1)S(1)}, u32[]{:S(2)}, u32[]{:S(2)}) %collective-permute-start) | collective-permute-done | bytes 262176 | tf_op jit(solution)/shard_map/while/body/eval_jaxpr/ppermute | solution.py:16
  196.7 4.5 %collective-permute-start = (bf16[512,256]{1,0:T(8,128)(2,1)}, bf16[512,256]{1,0:T(8,128)(2,1)S(1)}, u32[]{:S(2)}, u32[]{:S(2)}) collective-permute-start(bf16[512,256]{1,0:T(8,128)(2,1)} %get-tuple-element.190), channel_id=1, source_target_pairs={{0,8},{8,16},{16,24},{24,32},{32,40},{40,48},{48,56},{56,64},{64,7... | collective-permute-start | bytes 786440 | tf_op jit(solution)/shard_map/while/body/eval_jaxpr/ppermute | solution.py:16
  201.2 11.8 %collective-permute-done.1 = bf16[512,256]{1,0:T(8,128)(2,1)S(1)} collective-permute-done((bf16[512,256]{1,0:T(8,128)(2,1)}, bf16[512,256]{1,0:T(8,128)(2,1)S(1)}, u32[]{:S(2)}, u32[]{:S(2)}) %collective-permute-start.1) | collective-permute-done | bytes 262176 | tf_op jit(solution)/shard_map/while/body/eval_jaxpr/ppermute | solution.py:16
  221.3 3.9 %collective-permute-start = (bf16[512,256]{1,0:T(8,128)(2,1)}, bf16[512,256]{1,0:T(8,128)(2,1)S(1)}, u32[]{:S(2)}, u32[]{:S(2)}) collective-permute-start(bf16[512,256]{1,0:T(8,128)(2,1)} %get-tuple-element.190), channel_id=1, source_target_pairs={{0,8},{8,16},{16,24},{24,32},{32,40},{40,48},{48,56},{56,64},{64,7... | collective-permute-start | bytes 786440 | tf_op jit(solution)/shard_map/while/body/eval_jaxpr/ppermute | solution.py:16
  225.3 12.3 %collective-permute-done.1 = bf16[512,256]{1,0:T(8,128)(2,1)S(1)} collective-permute-done((bf16[512,256]{1,0:T(8,128)(2,1)}, bf16[512,256]{1,0:T(8,128)(2,1)S(1)}, u32[]{:S(2)}, u32[]{:S(2)}) %collective-permute-start.1) | collective-permute-done | bytes 262176 | tf_op jit(solution)/shard_map/while/body/eval_jaxpr/ppermute | solution.py:16
  244.5 4.1 %fusion.14 = bf16[4096,256]{0,1:T(8,128)(2,1)} fusion(bf16[4096,256]{0,1:T(8,128)(2,1)} %get-tuple-element.124, s32[]{:T(128)S(6)} %select_n.21, bf16[4096,256]{0,1:T(8,128)(2,1)} %copy.44), kind=kLoop, calls=%fused_computation.26 | loop fusion | flops 4194304 | bytes 6291460 | tf_op jit(solution)/shard_map/add | solution.py:83
  248.6 4.4 %fusion.15 = bf16[4096,256]{1,0:T(8,128)(2,1)} fusion(bf16[4096,256]{1,0:T(8,128)(2,1)S(1)} %copy-done.1, s32[]{:T(128)S(6)} %select_n.21, bf16[4096,256]{1,0:T(8,128)(2,1)S(1)} %copy-done.2), kind=kLoop, calls=%fused_computation.27 | loop fusion | flops 4194304 | bytes 6291460 | tf_op jit(solution)/shard_map/add | solution.py:82
  254.4 9.2 %fusion.4 = (f32[2,512]{1,0:T(2,128)S(1)}, f32[4608,512,2]{1,0,2:T(8,128)}) fusion(pred[512,4608]{0,1:T(8,128)(4,1)S(1)} %fusion.11, bf16[512,2,128]{0,2,1:T(8,128)(2,1)S(1)} %bitcast.106, bf16[4096,256]{1,0:T(8,128)(2,1)} %fusion.15, bf16[512,256]{1,0:T(8,128)(2,1)S(1)} %bitcast.100), kind=kOutput, calls=%fused_computation.10 | convolution fusion | flops 1224473600 | bytes 23859200 | tf_op jit(solution)/shard_map/while/body/eval_jaxpr/qgd,kd->gqk/dot_general | solution.py:42
  263.7 19.0 %fusion = (f32[2,512]{1,0:T(2,128)S(1)}, f32[2,512]{1,0:T(2,128)S(1)}, f32[4608,512,2]{1,0,2:T(8,128)}) fusion(f32[4608,512,2]{1,0,2:T(8,128)} %get-tuple-element.146, f32[2,512]{1,0:T(2,128)S(1)} %get-tuple-element.145, pred[512,4608]{0,1:T(8,128)(4,1)S(1)} %fusion.11, bf16[512,2,128]{0,2,1:T(8,128)(2,1)S(1)} %bitcast.105, ...), kind=kOutput, calls=%fused_computation.6 | convolution fusion | flops 1243346944 | bytes 42741760 | tf_op jit(solution)/shard_map/while/body/eval_jaxpr/qgd,kd->gqk/dot_general | solution.py:42
  282.7 9.8 %fusion.51 = bf16[512,2,128]{0,2,1:T(8,128)(2,1)S(1)} fusion(f32[4608,512,2]{1,0,2:T(8,128)} %get-tuple-element.146, f32[2,512]{1,0:T(2,128)S(1)} %get-tuple-element.145, pred[512,4608]{0,1:T(8,128)(4,1)S(1)} %fusion.11, bf16[4096,256]{0,1:T(8,128)(2,1)S(1)} %copy-done.3, bf16[512,256]{0,1:T(8,128)(2,1)S(1)} %copy-done.6, f32[512,2]{0,1:T(2,128)S(1)} %bitcast.108), kind=kOutput, calls=%fused_computation.45 | convolution fusion | flops 1229455360 | bytes 23863296 | tf_op jit(solution)/shard_map/while/body/eval_jaxpr/gqk,kd->qgd/dot_general | solution.py:50
  292.9 9.9 %fusion.2 = f32[2,512]{1,0:T(2,128)S(1)} fusion(f32[4608,512,2]{1,0,2:T(8,128)} %get-tuple-element.147, f32[2,512]{1,0:T(2,128)S(1)} %get-tuple-element.132, pred[512,4608]{0,1:T(8,128)(4,1)S(1)} %fusion.11), kind=kLoop, calls=%fused_computation.8 | loop fusion | flops 18873344 | bytes 21241856 | tf_op jit(solution)/shard_map/while/body/eval_jaxpr/reduce_sum | solution.py:48
  304.7 6.9 %fusion.41 = bf16[512,2,128]{0,2,1:T(8,128)(2,1)S(1)} fusion(f32[4608,512,2]{1,0,2:T(8,128)S(1)} %copy-done, f32[2,512]{1,0:T(2,128)S(1)} %get-tuple-element.132, pred[512,4608]{0,1:T(8,128)(4,1)S(1)} %fusion.11, bf16[512,256]{0,1:T(8,128)(2,1)S(1)} %copy-done.6, bf16[4096,256]{0,1:T(8,128)(2,1)} %fusion.14, f32[512,2]{0,1:T(2,128)S(1)} %bitcast.107), kind=kOutput, calls=%fused_computation.43 | convolution fusion | flops 1229455360 | bytes 23863296 | tf_op jit(solution)/shard_map/while/body/eval_jaxpr/gqk,kd->qgd/dot_general | solution.py:50
  312.0 69.0 %all_to_all.73 = bf16[8,64,512]{2,1,0:T(8,128)(2,1)S(1)} all-to-all(bf16[8,64,512]{2,1,0:T(8,128)(2,1)S(1)} %pad_maximum_fusion.2), channel_id=1, replica_groups=mesh['seq'=32,'head'=8] {'head'}, dimensions={0} | all-to-all | bytes 1048576 | tf_op jit(solution)/shard_map/all_to_all | solution.py:100
  (90 shorter events, 79.7 us)
Async XLA Ops:
  0.0 24.8 %copy-start.5 = (bf16[64,4096]{1,0:T(8,128)(2,1)S(1)}, bf16[64,4096]{1,0:T(8,128)(2,1)}, u32[]{:S(2)}) copy-start(bf16[64,4096]{1,0:T(8,128)(2,1)} %param.8) | copy-start | bytes 1572868
  1.7 15.8 %all-to-all-start.1 = ((bf16[64,8,256]{2,0,1:T(8,128)(2,1)}), bf16[64,8,256]{2,0,1:T(8,128)(2,1)}, u32[]{:S(2)}, u32[]{:S(2)}) async-start(bf16[64,8,256]{2,0,1:T(8,128)(2,1)} %bitcast.95), calls=%async_computation.1 | async-start | bytes 524288 | tf_op jit(solution)/shard_map/all_to_all | solution.py:61
  17.5 14.1 %all-to-all-start = ((bf16[64,8,256]{2,0,1:T(8,128)(2,1)}), bf16[64,8,256]{2,0,1:T(8,128)(2,1)S(1)}, u32[]{:S(2)}, u32[]{:S(2)}) async-start(bf16[64,8,256]{2,0,1:T(8,128)(2,1)} %bitcast.96), calls=%async_computation | async-start | bytes 524288 | tf_op jit(solution)/shard_map/all_to_all | solution.py:60
  31.5 221.5 %all-to-all-start.2 = ((bf16[64,8,512]{2,0,1:T(8,128)(2,1)}), bf16[64,8,512]{2,0,1:T(8,128)(2,1)}, u32[]{:S(2)}, u32[]{:S(2)}) async-start(bf16[64,8,512]{2,0,1:T(8,128)(2,1)} %bitcast.94), calls=%async_computation.2 | async-start | bytes 1048576 | tf_op jit(solution)/shard_map/all_to_all | solution.py:59
  40.3 21.0 %collective-permute-start.1 = (bf16[512,256]{1,0:T(8,128)(2,1)}, bf16[512,256]{1,0:T(8,128)(2,1)S(1)}, u32[]{:S(2)}, u32[]{:S(2)}) collective-permute-start(bf16[512,256]{1,0:T(8,128)(2,1)} %get-tuple-element.191), channel_id=1, source_target_pairs={{0,8},{8,16},{16,24},{24,32},{32,40},{40,48},{48,56},{56,64},{64,7... | collective-permute-start | bytes 786440 | tf_op jit(solution)/shard_map/while/body/eval_jaxpr/ppermute | solution.py:16
  47.4 22.2 %collective-permute-start = (bf16[512,256]{1,0:T(8,128)(2,1)}, bf16[512,256]{1,0:T(8,128)(2,1)S(1)}, u32[]{:S(2)}, u32[]{:S(2)}) collective-permute-start(bf16[512,256]{1,0:T(8,128)(2,1)} %get-tuple-element.190), channel_id=1, source_target_pairs={{0,8},{8,16},{16,24},{24,32},{32,40},{40,48},{48,56},{56,64},{64,7... | collective-permute-start | bytes 786440 | tf_op jit(solution)/shard_map/while/body/eval_jaxpr/ppermute | solution.py:16
  71.0 18.2 %collective-permute-start.1 = (bf16[512,256]{1,0:T(8,128)(2,1)}, bf16[512,256]{1,0:T(8,128)(2,1)S(1)}, u32[]{:S(2)}, u32[]{:S(2)}) collective-permute-start(bf16[512,256]{1,0:T(8,128)(2,1)} %get-tuple-element.191), channel_id=1, source_target_pairs={{0,8},{8,16},{16,24},{24,32},{32,40},{40,48},{48,56},{56,64},{64,7... | collective-permute-start | bytes 786440 | tf_op jit(solution)/shard_map/while/body/eval_jaxpr/ppermute | solution.py:16
  73.6 20.4 %collective-permute-start = (bf16[512,256]{1,0:T(8,128)(2,1)}, bf16[512,256]{1,0:T(8,128)(2,1)S(1)}, u32[]{:S(2)}, u32[]{:S(2)}) collective-permute-start(bf16[512,256]{1,0:T(8,128)(2,1)} %get-tuple-element.190), channel_id=1, source_target_pairs={{0,8},{8,16},{16,24},{24,32},{32,40},{40,48},{48,56},{56,64},{64,7... | collective-permute-start | bytes 786440 | tf_op jit(solution)/shard_map/while/body/eval_jaxpr/ppermute | solution.py:16
  95.5 18.3 %collective-permute-start.1 = (bf16[512,256]{1,0:T(8,128)(2,1)}, bf16[512,256]{1,0:T(8,128)(2,1)S(1)}, u32[]{:S(2)}, u32[]{:S(2)}) collective-permute-start(bf16[512,256]{1,0:T(8,128)(2,1)} %get-tuple-element.191), channel_id=1, source_target_pairs={{0,8},{8,16},{16,24},{24,32},{32,40},{40,48},{48,56},{56,64},{64,7... | collective-permute-start | bytes 786440 | tf_op jit(solution)/shard_map/while/body/eval_jaxpr/ppermute | solution.py:16
  97.4 20.2 %collective-permute-start = (bf16[512,256]{1,0:T(8,128)(2,1)}, bf16[512,256]{1,0:T(8,128)(2,1)S(1)}, u32[]{:S(2)}, u32[]{:S(2)}) collective-permute-start(bf16[512,256]{1,0:T(8,128)(2,1)} %get-tuple-element.190), channel_id=1, source_target_pairs={{0,8},{8,16},{16,24},{24,32},{32,40},{40,48},{48,56},{56,64},{64,7... | collective-permute-start | bytes 786440 | tf_op jit(solution)/shard_map/while/body/eval_jaxpr/ppermute | solution.py:16
  119.0 19.0 %collective-permute-start.1 = (bf16[512,256]{1,0:T(8,128)(2,1)}, bf16[512,256]{1,0:T(8,128)(2,1)S(1)}, u32[]{:S(2)}, u32[]{:S(2)}) collective-permute-start(bf16[512,256]{1,0:T(8,128)(2,1)} %get-tuple-element.191), channel_id=1, source_target_pairs={{0,8},{8,16},{16,24},{24,32},{32,40},{40,48},{48,56},{56,64},{64,7... | collective-permute-start | bytes 786440 | tf_op jit(solution)/shard_map/while/body/eval_jaxpr/ppermute | solution.py:16
  120.9 22.7 %collective-permute-start = (bf16[512,256]{1,0:T(8,128)(2,1)}, bf16[512,256]{1,0:T(8,128)(2,1)S(1)}, u32[]{:S(2)}, u32[]{:S(2)}) collective-permute-start(bf16[512,256]{1,0:T(8,128)(2,1)} %get-tuple-element.190), channel_id=1, source_target_pairs={{0,8},{8,16},{16,24},{24,32},{32,40},{40,48},{48,56},{56,64},{64,7... | collective-permute-start | bytes 786440 | tf_op jit(solution)/shard_map/while/body/eval_jaxpr/ppermute | solution.py:16
  145.1 18.2 %collective-permute-start.1 = (bf16[512,256]{1,0:T(8,128)(2,1)}, bf16[512,256]{1,0:T(8,128)(2,1)S(1)}, u32[]{:S(2)}, u32[]{:S(2)}) collective-permute-start(bf16[512,256]{1,0:T(8,128)(2,1)} %get-tuple-element.191), channel_id=1, source_target_pairs={{0,8},{8,16},{16,24},{24,32},{32,40},{40,48},{48,56},{56,64},{64,7... | collective-permute-start | bytes 786440 | tf_op jit(solution)/shard_map/while/body/eval_jaxpr/ppermute | solution.py:16
  147.0 21.1 %collective-permute-start = (bf16[512,256]{1,0:T(8,128)(2,1)}, bf16[512,256]{1,0:T(8,128)(2,1)S(1)}, u32[]{:S(2)}, u32[]{:S(2)}) collective-permute-start(bf16[512,256]{1,0:T(8,128)(2,1)} %get-tuple-element.190), channel_id=1, source_target_pairs={{0,8},{8,16},{16,24},{24,32},{32,40},{40,48},{48,56},{56,64},{64,7... | collective-permute-start | bytes 786440 | tf_op jit(solution)/shard_map/while/body/eval_jaxpr/ppermute | solution.py:16
  169.5 18.3 %collective-permute-start.1 = (bf16[512,256]{1,0:T(8,128)(2,1)}, bf16[512,256]{1,0:T(8,128)(2,1)S(1)}, u32[]{:S(2)}, u32[]{:S(2)}) collective-permute-start(bf16[512,256]{1,0:T(8,128)(2,1)} %get-tuple-element.191), channel_id=1, source_target_pairs={{0,8},{8,16},{16,24},{24,32},{32,40},{40,48},{48,56},{56,64},{64,7... | collective-permute-start | bytes 786440 | tf_op jit(solution)/shard_map/while/body/eval_jaxpr/ppermute | solution.py:16
  171.4 22.0 %collective-permute-start = (bf16[512,256]{1,0:T(8,128)(2,1)}, bf16[512,256]{1,0:T(8,128)(2,1)S(1)}, u32[]{:S(2)}, u32[]{:S(2)}) collective-permute-start(bf16[512,256]{1,0:T(8,128)(2,1)} %get-tuple-element.190), channel_id=1, source_target_pairs={{0,8},{8,16},{16,24},{24,32},{32,40},{40,48},{48,56},{56,64},{64,7... | collective-permute-start | bytes 786440 | tf_op jit(solution)/shard_map/while/body/eval_jaxpr/ppermute | solution.py:16
  194.8 18.2 %collective-permute-start.1 = (bf16[512,256]{1,0:T(8,128)(2,1)}, bf16[512,256]{1,0:T(8,128)(2,1)S(1)}, u32[]{:S(2)}, u32[]{:S(2)}) collective-permute-start(bf16[512,256]{1,0:T(8,128)(2,1)} %get-tuple-element.191), channel_id=1, source_target_pairs={{0,8},{8,16},{16,24},{24,32},{32,40},{40,48},{48,56},{56,64},{64,7... | collective-permute-start | bytes 786440 | tf_op jit(solution)/shard_map/while/body/eval_jaxpr/ppermute | solution.py:16
  196.7 21.3 %collective-permute-start = (bf16[512,256]{1,0:T(8,128)(2,1)}, bf16[512,256]{1,0:T(8,128)(2,1)S(1)}, u32[]{:S(2)}, u32[]{:S(2)}) collective-permute-start(bf16[512,256]{1,0:T(8,128)(2,1)} %get-tuple-element.190), channel_id=1, source_target_pairs={{0,8},{8,16},{16,24},{24,32},{32,40},{40,48},{48,56},{56,64},{64,7... | collective-permute-start | bytes 786440 | tf_op jit(solution)/shard_map/while/body/eval_jaxpr/ppermute | solution.py:16
  219.4 18.2 %collective-permute-start.1 = (bf16[512,256]{1,0:T(8,128)(2,1)}, bf16[512,256]{1,0:T(8,128)(2,1)S(1)}, u32[]{:S(2)}, u32[]{:S(2)}) collective-permute-start(bf16[512,256]{1,0:T(8,128)(2,1)} %get-tuple-element.191), channel_id=1, source_target_pairs={{0,8},{8,16},{16,24},{24,32},{32,40},{40,48},{48,56},{56,64},{64,7... | collective-permute-start | bytes 786440 | tf_op jit(solution)/shard_map/while/body/eval_jaxpr/ppermute | solution.py:16
  221.3 21.8 %collective-permute-start = (bf16[512,256]{1,0:T(8,128)(2,1)}, bf16[512,256]{1,0:T(8,128)(2,1)S(1)}, u32[]{:S(2)}, u32[]{:S(2)}) collective-permute-start(bf16[512,256]{1,0:T(8,128)(2,1)} %get-tuple-element.190), channel_id=1, source_target_pairs={{0,8},{8,16},{16,24},{24,32},{32,40},{40,48},{48,56},{56,64},{64,7... | collective-permute-start | bytes 786440 | tf_op jit(solution)/shard_map/while/body/eval_jaxpr/ppermute | solution.py:16
  244.5 4.1 %copy-start.1 = (bf16[4096,256]{1,0:T(8,128)(2,1)S(1)}, bf16[4096,256]{1,0:T(8,128)(2,1)}, u32[]{:S(2)}) copy-start(bf16[4096,256]{1,0:T(8,128)(2,1)} %get-tuple-element.125) | copy-start | bytes 6291460
  244.5 4.1 %copy-start.2 = (bf16[4096,256]{1,0:T(8,128)(2,1)S(1)}, bf16[4096,256]{1,0:T(8,128)(2,1)}, u32[]{:S(2)}) copy-start(bf16[4096,256]{1,0:T(8,128)(2,1)} %param.11) | copy-start | bytes 6291460
  254.4 9.3 %copy-start.4 = (bf16[4096,256]{1,0:T(8,128)(2,1)S(1)}, bf16[4096,256]{1,0:T(8,128)(2,1)}, u32[]{:S(2)}) copy-start(bf16[4096,256]{1,0:T(8,128)(2,1)} %fusion.15) | copy-start | bytes 6291460
  263.7 19.0 %copy-start.3 = (bf16[4096,256]{0,1:T(8,128)(2,1)S(1)}, bf16[4096,256]{0,1:T(8,128)(2,1)}, u32[]{:S(2)}) copy-start(bf16[4096,256]{0,1:T(8,128)(2,1)} %fusion.14) | copy-start | bytes 6291460
  263.7 19.0 %copy-start.6 = (bf16[512,256]{0,1:T(8,128)(2,1)S(1)}, bf16[512,256]{0,1:T(8,128)(2,1)}, u32[]{:S(2)}) copy-start(bf16[512,256]{0,1:T(8,128)(2,1)} %copy.46) | copy-start | bytes 786436
  292.9 11.8 %copy-start = (f32[4608,512,2]{1,0,2:T(8,128)S(1)}, f32[4608,512,2]{1,0,2:T(8,128)}, u32[]{:S(2)}) copy-start(f32[4608,512,2]{1,0,2:T(8,128)} %get-tuple-element.147) | copy-start | bytes 56623108
where the time goes:
time: 383 us; the launch traced here: 382 us
  waiting for transfers between devices  130 us (34%)
  starting transfers between devices  71.2 us (19%)
  blocking collectives  69 us (18%)
  matrix products  45 us (12%)
  local copies, waits for them, and re-layouts  42.9 us (11%)
  other arithmetic  22.3 us (6%)
    ppermute x16, waiting for transfers between devices, shifted(): return lax.ppermute(shard, axis, pairs)  123 us
    all_to_all x1, blocking collectives, shards(): lax.all_to_all(shortened(attended), 'head', split_axis=0, concat_axis=1,...  69 us
    ppermute x16, starting transfers between devices, shifted(): return lax.ppermute(shard, axis, pairs)  56.9 us
    dot_general x2, matrix products, attend_block(): jnp.einsum('qgd,kd->gqk', query_head, key_head, preferred_element_type=jn...  28.2 us
    dot_general x2, matrix products, attend_block(): jnp.einsum('gqk,kd->qgd', weights, value_head, preferred_element_type=jnp...  16.8 us
    while x16, local copies, waits for them, and re-layouts  11.3 us
    reduce_sum x1, other arithmetic, attend_block(): totals = jnp.sum(unnormed, axis=2)  9.86 us
  transfers between devices with their start and end apart: 19, of which 17 were waited for; matrix products, arithmetic and copies ran while one was open for 13% of the time, Pallas kernels for 0%

commit v1 on v0

v1 whole, which is shorter than its diff:
```python
import functools
import math

import jax
import jax.numpy as jnp
from jax import lax
from jax.experimental import pallas as pl
from jax.experimental.pallas import tpu as pltpu
from jax.sharding import PartitionSpec as P

HEAD_DIM = 128
QH = 32
KVH = 16
QSCALE = 144
WINDOW = 4096

MESH = pl.DeviceIdType.MESH
ROWS = 64
COLUMN = 1024
PIECE = 256
PIECES = COLUMN // PIECE
SLOTS = 5
SPAN = WINDOW + PIECE
STEPS = SPAN // PIECE
PAIR = 2 * HEAD_DIM
MASKED = -1e30
LOG2E_SCALED = math.log2(math.e) * QSCALE ** (-0.5)
NT = (((1,), (1,)), ((), ()))


def ring_offset(t):
    half = (t + 1) // 2
    return jnp.where(t % 2 == 1, half, -half)


def kernel(
    start_ref, q_ref, k_ref, v_ref, pk_ref, pv_ref, out_ref,
    window, q_in, keys2, values2, q2, scores, peaks, o_out,
    kv_sem, q_sem, o_sem, in_send, fwd_send, prefix_send, o_send,
):
    seq, head = lax.axis_index("seq"), lax.axis_index("head")
    y, x, z = seq // 8, (seq // 2) % 4, (seq % 2) * 4 + head // 2
    core = head % 2
    z_hi = seq % 2
    xp, xl = x // 2, x % 2
    other = 1 - core
    my_column = 2 * xp + core
    flip = (xl + xp) % 2

    def device(y_, x_, z_, core_):
        return (y_ * 8 + x_ * 2 + z_ // 4, (z_ % 4) * 2 + core_)

    def chip_head(x_, z_):
        return (z_ % 4) * 4 + (z_ // 4) * 2 + (x_ % 2 + x_ // 2) % 2

    my_head = chip_head(x, z)
    x_near = 3 - x

    def remote(src, dst, send, recv, to):
        return pltpu.make_async_remote_copy(
            src_ref=src, dst_ref=dst, send_sem=send, recv_sem=recv,
            device_id=to, device_id_type=MESH,
        )

    barrier = pltpu.get_barrier_semaphore()

    def greet(to):
        pl.semaphore_signal(barrier, inc=1, device_id=to, device_id_type=MESH)

    def greet_group(i, carry):
        x_, z_, core_ = 2 * xp + i // 16, (i // 2) % 8, i % 2
        pl.when(jnp.logical_not((x_ == x) & (z_ == z) & (core_ == core)))(
            lambda: greet(device(y, x_, z_, core_))
        )
        return carry

    lax.fori_loop(0, 32, greet_group, 0)
    greet(device(y, x_near, z, core))
    greet(device((y + 1) % 4, x, z, core))
    greet(device((y + 3) % 4, x, z, core))
    pl.semaphore_wait(barrier, 34)

    my_rows = pl.ds(pl.multiple_of((z * 2 + core) * ROWS, ROWS), ROWS)

    def each_target(body):
        def at(t, carry):
            z_ = (z + ring_offset(t) + 8) % 8
            for lane in range(2):
                x_ = 2 * xp + lane
                mine = (t == 0) & (xl == lane) & (core == xl)
                body(t, lane, x_, z_, mine)
            return carry

        lax.fori_loop(0, 8, at, 0)

    def send_kv(t, lane, x_, z_, mine):
        h = chip_head(x_, z_)
        cols = pl.ds(pl.multiple_of(h * HEAD_DIM, HEAD_DIM), HEAD_DIM)
        for n, src in enumerate((k_ref, v_ref)):
            dst = window.at[4, my_rows, pl.ds(n * HEAD_DIM, HEAD_DIM)]
            recv = kv_sem.at[4, z // 2]

            @pl.when(mine)
            def _():
                pltpu.make_async_copy(src.at[:, cols], dst, recv).start()

            @pl.when(jnp.logical_not(mine))
            def _():
                remote(
                    src.at[:, cols], dst, in_send.at[t, lane, n], recv, device(y, x_, z_, xl)
                ).start()

    def send_q(t, lane, x_, z_, mine):
        h = chip_head(x_, z_)
        cols = pl.ds(pl.multiple_of(h * PAIR, PAIR), PAIR)
        dst = q_in.at[my_rows, :]
        recv = q_sem.at[z // 2]

        @pl.when(mine)
        def _():
            pltpu.make_async_copy(q_ref.at[:, cols], dst, recv).start()

        @pl.when(jnp.logical_not(mine))
        def _():
            remote(
                q_ref.at[:, cols], dst, in_send.at[t, lane, 2], recv, device(y, x_, z_, xl)
            ).start()

    def sent(t, lane, x_, z_, mine):
        @pl.when(jnp.logical_not(mine))
        def _():
            to = device(y, x_, z_, xl)
            for n, src in enumerate((k_ref, v_ref)):
                cols = pl.ds(0, HEAD_DIM)
                dst = window.at[4, my_rows, pl.ds(n * HEAD_DIM, HEAD_DIM)]
                remote(src.at[:, cols], dst, in_send.at[t, lane, n], kv_sem.at[4, 0], to).wait_send()
            remote(
                q_ref.at[:, pl.ds(0, PAIR)], q_in.at[my_rows, :], in_send.at[t, lane, 2], q_sem.at[0], to
            ).wait_send()

    each_target(send_kv)

    def prefix_copies(p, mine):
        whose = core if mine else other
        rows = pl.ds(pl.multiple_of((2 * xp + whose) * COLUMN + p * PIECE, PIECE), PIECE)
        cols = pl.ds(pl.multiple_of(flip * HEAD_DIM, HEAD_DIM), HEAD_DIM)
        for n, src in enumerate((pk_ref, pv_ref)):
            dst = window.at[0, pl.ds(p * PIECE, PIECE), pl.ds(n * HEAD_DIM, HEAD_DIM)]
            if mine:
                yield pltpu.make_async_copy(src.at[rows, cols], dst, kv_sem.at[0, p])
            else:
                yield remote(
                    src.at[rows, cols], dst, prefix_send.at[p, n], kv_sem.at[0, p],
                    device(y, x, z, other),
                )

    has_prefix = (y == 0) & (core == z_hi)

    @pl.when(has_prefix)
    def _():
        for p in range(PIECES):
            for mine in (True, False):
                for copy in prefix_copies(p, mine):
                    copy.start()

    each_target(send_q)

    def piece_at(i):
        return (z // 2 + ring_offset(i) + 4) % 4

    def routes(slot):
        across = device(y, x, z, other)
        near = device(y, x_near, z, core)
        if slot == 4:
            return (
                (y < 3, device((y + 1) % 4, x, z, core), 0, 0),
                (xp == 0, near, 2, 1),
                (core == 0, across, 3, 2),
            )
        if slot == 0:
            return ((xp == 1, near, 2, 1), (core == 1, across, 1, 3))
        return ((core == 0, across, 1, 3), (core == 1, across, 3, 2))

    def arrived(slot, p):
        rows = pl.ds(pl.multiple_of(p * PIECE, PIECE), PIECE)
        ref = window.at[slot, rows, :]
        pltpu.make_async_copy(ref, ref, kv_sem.at[slot, p]).wait()

    def forward(slot, p, start):
        rows = pl.ds(pl.multiple_of(p * PIECE, PIECE), PIECE)
        for condition, to, there, n in routes(slot):

            @pl.when(condition)
            def _():
                copy = remote(
                    window.at[slot, rows, :], window.at[there, rows, :],
                    fwd_send.at[n, p], kv_sem.at[there, p], to,
                )
                copy.start() if start else copy.wait_send()

    order = sorted((i + d, d, slot, i) for d, slot in enumerate((4, 0, 2)) for i in range(PIECES))
    for _, _, slot, i in order:
        p = piece_at(i)
        arrived(slot, p)
        forward(slot, p, True)
    for slot in (1, 3):
        for p in range(PIECES):
            arrived(slot, p)

    first_row = WINDOW - (4 * y + my_column) * COLUMN - start_ref[0]
    spare = window[4, 0:1, 0:HEAD_DIM].astype(jnp.float32)

    def build(i, carry):
        slot, p = i // PIECES, i % PIECES
        rows = pl.ds(pl.multiple_of(p * PIECE, PIECE), PIECE)
        at = pl.ds(pl.multiple_of(i * PIECE, PIECE), PIECE)
        row = i * PIECE + lax.broadcasted_iota(jnp.int32, (PIECE, HEAD_DIM), 0)
        real = row >= first_row
        k = jnp.where(real, window[slot, rows, 0:HEAD_DIM].astype(jnp.float32), spare)
        v = jnp.where(real, window[slot, rows, HEAD_DIM:PAIR].astype(jnp.float32), 0.0)
        k = k.astype(jnp.bfloat16)
        keys2[at, 0:HEAD_DIM] = k
        keys2[at, HEAD_DIM:PAIR] = k
        values2[at, 0:HEAD_DIM] = v.astype(jnp.bfloat16)
        values2[at, HEAD_DIM:PAIR] = jnp.where(real, 1.0, 0.0).astype(jnp.bfloat16)
        return carry

    lax.fori_loop(0, SLOTS * PIECES, build, 0)

    def queries(i):
        p = piece_at(i)
        rows = pl.ds(pl.multiple_of(p * PIECE, PIECE), PIECE)
        ref = q_in.at[rows, :]
        pltpu.make_async_copy(ref, ref, q_sem.at[p]).wait()
        for h in range(2):
            scaled = q_in[rows, h * HEAD_DIM : (h + 1) * HEAD_DIM].astype(jnp.float32) * LOG2E_SCALED
            high = scaled.astype(jnp.bfloat16)
            q2[h * PIECE : (h + 1) * PIECE, 0:HEAD_DIM] = high
            q2[h * PIECE : (h + 1) * PIECE, HEAD_DIM:PAIR] = (
                scaled - high.astype(jnp.float32)
            ).astype(jnp.bfloat16)

    def score(i, slot, step, peak):
        p = piece_at(i)
        at = pl.ds(pl.multiple_of((p + step) * PIECE, PIECE), PIECE)
        s = lax.dot_general(q2[...], keys2[at, :], NT, preferred_element_type=jnp.float32)
        if step in (0, STEPS - 1):
            token = lax.broadcasted_iota(jnp.int32, s.shape, 0) % PIECE
            key = lax.broadcasted_iota(jnp.int32, s.shape, 1)
            s = jnp.where(key > token if step == 0 else key <= token, s, MASKED)
        scores[slot, :, step * PIECE : (step + 1) * PIECE] = s
        for lane in range(0, PIECE, HEAD_DIM):
            peak = jnp.maximum(peak, s[:, lane : lane + HEAD_DIM])
        return peak

    def no_peak():
        return jnp.full((2 * PIECE, HEAD_DIM), MASKED, jnp.float32)

    def keep_peak(slot, peak):
        peaks[slot] = jnp.broadcast_to(jnp.max(peak, axis=1, keepdims=True), peak.shape)

    def mix(i, slot, step):
        p = piece_at(i)
        at = pl.ds(pl.multiple_of((p + step) * PIECE, PIECE), PIECE)
        peak = peaks[slot]
        weights = [
            jnp.exp2(scores[slot, :, lane : lane + HEAD_DIM] - peak).astype(jnp.bfloat16)
            for lane in range(step * PIECE, (step + 1) * PIECE, HEAD_DIM)
        ]
        return jnp.dot(
            jnp.concatenate(weights, axis=1), values2[at, :], preferred_element_type=jnp.float32
        )

    def home_copies(i, start):
        p = piece_at(i)
        cols = pl.ds(pl.multiple_of(my_head * PAIR, PAIR), PAIR)
        for n in range(4):
            z_, core_ = 2 * p + n // 2, n % 2
            mine = (my_column == x) & (z_ == z) & (core_ == core)
            src = o_out.at[p, pl.ds(n * ROWS, ROWS), :]
            dst = out_ref.at[:, cols]

            @pl.when(mine)
            def _():
                if start:
                    pltpu.make_async_copy(src, dst, o_sem).start()

            @pl.when(jnp.logical_not(mine))
            def _():
                copy = remote(src, dst, o_send.at[p, n], o_sem, device(y, my_column, z_, core_))
                copy.start() if start else copy.wait_send()

    def finish(i, total):
        p = piece_at(i)
        o = total[:, 0:HEAD_DIM] / total[:, HEAD_DIM:PAIR]
        o_out[p, :, 0:HEAD_DIM] = o[0:PIECE].astype(jnp.bfloat16)
        o_out[p, :, HEAD_DIM:PAIR] = o[PIECE:].astype(jnp.bfloat16)
        home_copies(i, True)

    queries(0)
    peak = no_peak()
    for step in range(STEPS):
        peak = score(0, 0, step, peak)
    keep_peak(0, peak)

    def piece(i, carry):
        slot = i % 2
        queries(i + 1)
        peak = no_peak()
        total = None
        for step in range(STEPS):
            peak = score(i + 1, 1 - slot, step, peak)
            part = mix(i, slot, step)
            total = part if total is None else total + part
        keep_peak(1 - slot, peak)
        finish(i, total)
        return carry

    lax.fori_loop(0, PIECES - 1, piece, 0)
    total = None
    for step in range(STEPS):
        part = mix(PIECES - 1, (PIECES - 1) % 2, step)
        total = part if total is None else total + part
    finish(PIECES - 1, total)

    pltpu.make_async_copy(out_ref, out_ref, o_sem).wait()
    each_target(sent)

    @pl.when(has_prefix)
    def _():
        for p in range(PIECES):
            for copy in prefix_copies(p, False):
                copy.wait_send()

    for slot in (4, 0, 2):
        for p in range(PIECES):
            forward(slot, p, False)
    for i in range(PIECES):
        home_copies(i, False)


def shards(queries, keys, values, prefix_keys, prefix_values, span_start):
    anywhere = pl.BlockSpec(memory_space=pl.ANY)
    return pl.pallas_call(
        kernel,
        out_shape=jax.ShapeDtypeStruct(queries.shape, jnp.bfloat16),
        in_specs=[pl.BlockSpec(memory_space=pltpu.SMEM)] + [anywhere] * 5,
        out_specs=anywhere,
        scratch_shapes=[
            pltpu.VMEM((SLOTS, COLUMN, PAIR), jnp.bfloat16),
            pltpu.VMEM((COLUMN, PAIR), jnp.bfloat16),
            pltpu.VMEM((SLOTS * COLUMN, PAIR), jnp.bfloat16),
            pltpu.VMEM((SLOTS * COLUMN, PAIR), jnp.bfloat16),
            pltpu.VMEM((2 * PIECE, PAIR), jnp.bfloat16),
            pltpu.VMEM((2, 2 * PIECE, SPAN), jnp.float32),
            pltpu.VMEM((2, 2 * PIECE, HEAD_DIM), jnp.float32),
            pltpu.VMEM((PIECES, PIECE, PAIR), jnp.bfloat16),
            pltpu.SemaphoreType.DMA((SLOTS, PIECES)),
            pltpu.SemaphoreType.DMA((PIECES,)),
            pltpu.SemaphoreType.DMA,
            pltpu.SemaphoreType.DMA((8, 2, 3)),
            pltpu.SemaphoreType.DMA((4, PIECES)),
            pltpu.SemaphoreType.DMA((PIECES, 2)),
            pltpu.SemaphoreType.DMA((PIECES, 4)),
        ],
        compiler_params=pltpu.CompilerParams(
            collective_id=0, has_side_effects=True, vmem_limit_bytes=60 << 20
        ),
    )(span_start, queries, keys, values, prefix_keys, prefix_values)


def solution(mesh):
    placed = (
        P(("seq", "head"), None),
        P(("seq", "head"), None),
        P(("seq", "head"), None),
        P(None, "head"),
        P(None, "head"),
        P(),
    )
    return jax.shard_map(
        shards, mesh=mesh, in_specs=placed, out_specs=P(("seq", "head"), None), check_vma=False
    )
```

time: 383 us -> 72.1 us (0.19)
  the two profiles are of different devices: /device:TPU:16 before, /device:TPU:43 now
where the time goes in v1:
time: 72.1 us; the launch traced here: 71.9 us
  Pallas kernels  69.4 us (96%)
  local copies, waits for them, and re-layouts  1.87 us (3%)
    pallas_call x1, Pallas kernels, shards(): pl.pallas_call(kernel, out_shape=jax.ShapeDtypeStruct(queries.shape, jnp....  69.4 us
    unnamed x1, local copies, waits for them, and re-layouts  1.87 us

profile of v1, /device:TPU:43, one launch (start us, length us, event | category | flops | bytes accessed | tf_op | source)
XLA Modules:
  0.0 71.9 jit_solution(6581606141938774979)
XLA Ops:
  0.7 69.4 %shard_map.64 = bf16[64,4096]{1,0:T(8,128)(2,1)} custom-call(s32[1]{0:T(128)S(6)} %copy.8.start_ref, bf16[64,4096]{1,0:T(8,128)(2,1)} %q_ref.1, bf16[64,2048]{1,0:T(8,128)(2,1)} %k_ref.1, bf16[64,2048]{1,0:T(8,128)(2,1)} %v_ref.1, bf16[4096,256]{1,0:T(8,128)(2,1)} %pk_ref.1, bf16[4096,256]{1,0:T(8,128)(2,1)} %pv_ref.1), custom_call_target="tpu_custom_call" | custom-call | tf_op jit(solution)/shard_map/pallas_call | solution.py:344
  70.1 1.9 %copy.9 = bf16[64,4096]{1,0:T(8,128)(2,1)} copy(bf16[64,4096]{1,0:T(8,128)(2,1)} %shard_map.64) | data formatting | bytes 1048576

commit v2 on v1

--- a/solution.py
+++ b/solution.py
@@ -19,6 +19,8 @@
 COLUMN = 1024
 PIECE = 256
 PIECES = COLUMN // PIECE
+CHIP = 128
+CHIPS = COLUMN // CHIP
 SLOTS = 5
 SPAN = WINDOW + PIECE
 STEPS = SPAN // PIECE
@@ -29,6 +31,7 @@
 
 
 def ring_offset(t):
+    t = (8 - t) % 8
     half = (t + 1) // 2
     return jnp.where(t % 2 == 1, half, -half)
 
@@ -78,6 +81,7 @@
     greet(device(y, x_near, z, core))
     greet(device((y + 1) % 4, x, z, core))
     greet(device((y + 3) % 4, x, z, core))
+    values2[:, HEAD_DIM:PAIR] = jnp.ones((SLOTS * COLUMN, HEAD_DIM), jnp.bfloat16)
     pl.semaphore_wait(barrier, 34)
 
     my_rows = pl.ds(pl.multiple_of((z * 2 + core) * ROWS, ROWS), ROWS)
@@ -98,7 +102,7 @@
         cols = pl.ds(pl.multiple_of(h * HEAD_DIM, HEAD_DIM), HEAD_DIM)
         for n, src in enumerate((k_ref, v_ref)):
             dst = window.at[4, my_rows, pl.ds(n * HEAD_DIM, HEAD_DIM)]
-            recv = kv_sem.at[4, z // 2]
+            recv = kv_sem.at[4, z]
 
             @pl.when(mine)
             def _():
@@ -142,10 +146,10 @@
 
     def prefix_copies(p, mine):
         whose = core if mine else other
-        rows = pl.ds(pl.multiple_of((2 * xp + whose) * COLUMN + p * PIECE, PIECE), PIECE)
+        rows = pl.ds(pl.multiple_of((2 * xp + whose) * COLUMN + p * CHIP, CHIP), CHIP)
         cols = pl.ds(pl.multiple_of(flip * HEAD_DIM, HEAD_DIM), HEAD_DIM)
         for n, src in enumerate((pk_ref, pv_ref)):
-            dst = window.at[0, pl.ds(p * PIECE, PIECE), pl.ds(n * HEAD_DIM, HEAD_DIM)]
+            dst = window.at[0, pl.ds(p * CHIP, CHIP), pl.ds(n * HEAD_DIM, HEAD_DIM)]
             if mine:
                 yield pltpu.make_async_copy(src.at[rows, cols], dst, kv_sem.at[0, p])
             else:
@@ -158,15 +162,17 @@
 
     @pl.when(has_prefix)
     def _():
-        for p in range(PIECES):
+        for p in range(CHIPS):
             for mine in (True, False):
                 for copy in prefix_copies(p, mine):
                     copy.start()
 
     each_target(send_q)
 
+    toward = jnp.where(z % 2 == 0, 1, 3)
+
     def piece_at(i):
-        return (z // 2 + ring_offset(i) + 4) % 4
+        return (z // 2 + jnp.where(i == 0, 2, jnp.where(i == 1, toward, jnp.where(i == 2, -toward, 0))) + 4) % 4
 
     def routes(slot):
         across = device(y, x, z, other)
@@ -182,12 +188,12 @@
         return ((core == 0, across, 1, 3), (core == 1, across, 3, 2))
 
     def arrived(slot, p):
-        rows = pl.ds(pl.multiple_of(p * PIECE, PIECE), PIECE)
+        rows = pl.ds(pl.multiple_of(p * CHIP, CHIP), CHIP)
         ref = window.at[slot, rows, :]
         pltpu.make_async_copy(ref, ref, kv_sem.at[slot, p]).wait()
 
     def forward(slot, p, start):
-        rows = pl.ds(pl.multiple_of(p * PIECE, PIECE), PIECE)
+        rows = pl.ds(pl.multiple_of(p * CHIP, CHIP), CHIP)
         for condition, to, there, n in routes(slot):
 
             @pl.when(condition)
@@ -198,34 +204,54 @@
                 )
                 copy.start() if start else copy.wait_send()
 
-    order = sorted((i + d, d, slot, i) for d, slot in enumerate((4, 0, 2)) for i in range(PIECES))
-    for _, _, slot, i in order:
-        p = piece_at(i)
-        arrived(slot, p)
-        forward(slot, p, True)
-    for slot in (1, 3):
-        for p in range(PIECES):
-            arrived(slot, p)
-
-    first_row = WINDOW - (4 * y + my_column) * COLUMN - start_ref[0]
-    spare = window[4, 0:1, 0:HEAD_DIM].astype(jnp.float32)
-
-    def build(i, carry):
-        slot, p = i // PIECES, i % PIECES
-        rows = pl.ds(pl.multiple_of(p * PIECE, PIECE), PIECE)
-        at = pl.ds(pl.multiple_of(i * PIECE, PIECE), PIECE)
-        row = i * PIECE + lax.broadcasted_iota(jnp.int32, (PIECE, HEAD_DIM), 0)
-        real = row >= first_row
-        k = jnp.where(real, window[slot, rows, 0:HEAD_DIM].astype(jnp.float32), spare)
-        v = jnp.where(real, window[slot, rows, HEAD_DIM:PAIR].astype(jnp.float32), 0.0)
-        k = k.astype(jnp.bfloat16)
+    def build(slot, p):
+        rows = pl.ds(pl.multiple_of(p * CHIP, CHIP), CHIP)
+        at = pl.ds(pl.multiple_of(slot * COLUMN + p * CHIP, CHIP), CHIP)
+        k = window[slot, rows, 0:HEAD_DIM]
         keys2[at, 0:HEAD_DIM] = k
         keys2[at, HEAD_DIM:PAIR] = k
-        values2[at, 0:HEAD_DIM] = v.astype(jnp.bfloat16)
-        values2[at, HEAD_DIM:PAIR] = jnp.where(real, 1.0, 0.0).astype(jnp.bfloat16)
+        values2[at, 0:HEAD_DIM] = window[slot, rows, HEAD_DIM:PAIR]
+
+    def relay(i, carry):
+        for lag, slot in ((0, 4), (2, 0), (4, 2)):
+
+            @pl.when((i >= lag) & (i < lag + CHIPS))
+            def _():
+                p = (z - ring_offset(i - lag) + 8) % 8
+                arrived(slot, p)
+                forward(slot, p, True)
+                build(slot, p)
+
         return carry
 
-    lax.fori_loop(0, SLOTS * PIECES, build, 0)
+    lax.fori_loop(0, CHIPS + 4, relay, 0)
+
+    def last(i, carry):
+        for slot in (3, 1):
+            p = (z - ring_offset(i) + 8) % 8
+            arrived(slot, p)
+            build(slot, p)
+        return carry
+
+    lax.fori_loop(0, CHIPS, last, 0)
+
+    @pl.when(y == 0)
+    def _():
+        first_row = WINDOW - my_column * COLUMN - start_ref[0]
+        spare = window[4, 0:1, 0:HEAD_DIM].astype(jnp.float32)
+
+        def fix(i, carry):
+            at = pl.ds(pl.multiple_of(i * PIECE, PIECE), PIECE)
+            real = i * PIECE + lax.broadcasted_iota(jnp.int32, (PIECE, HEAD_DIM), 0) >= first_row
+            k = jnp.where(real, keys2[at, 0:HEAD_DIM].astype(jnp.float32), spare).astype(jnp.bfloat16)
+            v = jnp.where(real, values2[at, 0:HEAD_DIM].astype(jnp.float32), 0.0)
+            keys2[at, 0:HEAD_DIM] = k
+            keys2[at, HEAD_DIM:PAIR] = k
+            values2[at, 0:HEAD_DIM] = v.astype(jnp.bfloat16)
+            values2[at, HEAD_DIM:PAIR] = jnp.where(real, 1.0, 0.0).astype(jnp.bfloat16)
+            return carry
+
+        lax.fori_loop(0, WINDOW // PIECE, fix, 0)
 
     def queries(i):
         p = piece_at(i)
@@ -328,13 +354,16 @@
 
     @pl.when(has_prefix)
     def _():
-        for p in range(PIECES):
+        for p in range(CHIPS):
             for copy in prefix_copies(p, False):
                 copy.wait_send()
 
-    for slot in (4, 0, 2):
-        for p in range(PIECES):
+    def forwarded(p, carry):
+        for slot in (4, 0, 2):
             forward(slot, p, False)
+        return carry
+
+    lax.fori_loop(0, CHIPS, forwarded, 0)
     for i in range(PIECES):
         home_copies(i, False)
 
@@ -355,12 +384,12 @@
             pltpu.VMEM((2, 2 * PIECE, SPAN), jnp.float32),
             pltpu.VMEM((2, 2 * PIECE, HEAD_DIM), jnp.float32),
             pltpu.VMEM((PIECES, PIECE, PAIR), jnp.bfloat16),
-            pltpu.SemaphoreType.DMA((SLOTS, PIECES)),
+            pltpu.SemaphoreType.DMA((SLOTS, CHIPS)),
             pltpu.SemaphoreType.DMA((PIECES,)),
             pltpu.SemaphoreType.DMA,
             pltpu.SemaphoreType.DMA((8, 2, 3)),
-            pltpu.SemaphoreType.DMA((4, PIECES)),
-            pltpu.SemaphoreType.DMA((PIECES, 2)),
+            pltpu.SemaphoreType.DMA((4, CHIPS)),
+            pltpu.SemaphoreType.DMA((CHIPS, 2)),
             pltpu.SemaphoreType.DMA((PIECES, 4)),
         ],
         compiler_params=pltpu.CompilerParams(

time: 72.1 us -> 62.8 us (0.87)
  the two profiles are of different devices: /device:TPU:43 before, /device:TPU:33 now
where the time goes in v2:
time: 62.8 us; the launch traced here: 61.7 us
  Pallas kernels  59.2 us (94%)
  local copies, waits for them, and re-layouts  1.87 us (3%)
  between operations  0.66 us (1%)
    pallas_call x1, Pallas kernels, shards(): pl.pallas_call(kernel, out_shape=jax.ShapeDtypeStruct(queries.shape, jnp....  59.2 us
    unnamed x1, local copies, waits for them, and re-layouts  1.87 us

profile of v2, /device:TPU:33, one launch (start us, length us, event | category | flops | bytes accessed | tf_op | source)
XLA Modules:
  0.0 61.7 jit_solution(1786203661630134134)
XLA Ops:
  0.7 59.2 %shard_map.64 = bf16[64,4096]{1,0:T(8,128)(2,1)} custom-call(s32[1]{0:T(128)S(6)} %copy.8.start_ref, bf16[64,4096]{1,0:T(8,128)(2,1)} %q_ref.1, bf16[64,2048]{1,0:T(8,128)(2,1)} %k_ref.1, bf16[64,2048]{1,0:T(8,128)(2,1)} %v_ref.1, bf16[4096,256]{1,0:T(8,128)(2,1)} %pk_ref.1, bf16[4096,256]{1,0:T(8,128)(2,1)} %pv_ref.1), custom_call_target="tpu_custom_call" | custom-call | tf_op jit(solution)/shard_map/pallas_call | solution.py:373
  59.9 1.9 %copy.9 = bf16[64,4096]{1,0:T(8,128)(2,1)} copy(bf16[64,4096]{1,0:T(8,128)(2,1)} %shard_map.64) | data formatting | bytes 1048576

commit v3 on v2

--- a/solution.py
+++ b/solution.py
@@ -14,13 +14,14 @@
 QSCALE = 144
 WINDOW = 4096
 
-MESH = pl.DeviceIdType.MESH
+LOGICAL = pl.DeviceIdType.LOGICAL
 ROWS = 64
 COLUMN = 1024
 PIECE = 256
 PIECES = COLUMN // PIECE
 CHIP = 128
 CHIPS = COLUMN // CHIP
+AHEAD = 8
 SLOTS = 5
 SPAN = WINDOW + PIECE
 STEPS = SPAN // PIECE
@@ -31,14 +32,13 @@
 
 
 def ring_offset(t):
-    t = (8 - t) % 8
     half = (t + 1) // 2
     return jnp.where(t % 2 == 1, half, -half)
 
 
 def kernel(
     start_ref, q_ref, k_ref, v_ref, pk_ref, pv_ref, out_ref,
-    window, q_in, keys2, values2, q2, scores, peaks, o_out,
+    window, q_in, keys2, values2, q2, even_scores, odd_scores, even_peaks, odd_peaks, o_out,
     kv_sem, q_sem, o_sem, in_send, fwd_send, prefix_send, o_send,
 ):
     seq, head = lax.axis_index("seq"), lax.axis_index("head")
@@ -51,7 +51,7 @@
     flip = (xl + xp) % 2
 
     def device(y_, x_, z_, core_):
-        return (y_ * 8 + x_ * 2 + z_ // 4, (z_ % 4) * 2 + core_)
+        return y_ * 64 + x_ * 16 + z_ * 2 + core_
 
     def chip_head(x_, z_):
         return (z_ % 4) * 4 + (z_ // 4) * 2 + (x_ % 2 + x_ // 2) % 2
@@ -62,22 +62,19 @@
     def remote(src, dst, send, recv, to):
         return pltpu.make_async_remote_copy(
             src_ref=src, dst_ref=dst, send_sem=send, recv_sem=recv,
-            device_id=to, device_id_type=MESH,
+            device_id=to, device_id_type=LOGICAL,
         )
 
     barrier = pltpu.get_barrier_semaphore()
 
     def greet(to):
-        pl.semaphore_signal(barrier, inc=1, device_id=to, device_id_type=MESH)
-
-    def greet_group(i, carry):
-        x_, z_, core_ = 2 * xp + i // 16, (i // 2) % 8, i % 2
-        pl.when(jnp.logical_not((x_ == x) & (z_ == z) & (core_ == core)))(
-            lambda: greet(device(y, x_, z_, core_))
-        )
-        return carry
-
-    lax.fori_loop(0, 32, greet_group, 0)
+        pl.semaphore_signal(barrier, inc=1, device_id=to, device_id_type=LOGICAL)
+
+    group = device(y, 2 * xp, 0, 0)
+    place = device(0, xl, z, core)
+    for i in range(16, 48):
+        if i != 32:
+            greet(group + lax.rem(place + i, 32))
     greet(device(y, x_near, z, core))
     greet(device((y + 1) % 4, x, z, core))
     greet(device((y + 3) % 4, x, z, core))
@@ -86,16 +83,19 @@
 
     my_rows = pl.ds(pl.multiple_of((z * 2 + core) * ROWS, ROWS), ROWS)
 
-    def each_target(body):
+    def targets(body, t):
+        z_ = (z + ring_offset(t) + 8) % 8
+        for lane in range(2):
+            x_ = 2 * xp + lane
+            mine = (t == 0) & (xl == lane) & (core == xl)
+            body(t, lane, x_, z_, mine)
+
+    def each_target(body, first=0, stop=8):
         def at(t, carry):
-            z_ = (z + ring_offset(t) + 8) % 8
-            for lane in range(2):
-                x_ = 2 * xp + lane
-                mine = (t == 0) & (xl == lane) & (core == xl)
-                body(t, lane, x_, z_, mine)
+            targets(body, t)
             return carry
 
-        lax.fori_loop(0, 8, at, 0)
+        lax.fori_loop(first, stop, at, 0)
 
     def send_kv(t, lane, x_, z_, mine):
         h = chip_head(x_, z_)
@@ -142,7 +142,7 @@
                 q_ref.at[:, pl.ds(0, PAIR)], q_in.at[my_rows, :], in_send.at[t, lane, 2], q_sem.at[0], to
             ).wait_send()
 
-    each_target(send_kv)
+    each_target(send_kv, 0, AHEAD)
 
     def prefix_copies(p, mine):
         whose = core if mine else other
@@ -167,8 +167,6 @@
                 for copy in prefix_copies(p, mine):
                     copy.start()
 
-    each_target(send_q)
-
     toward = jnp.where(z % 2 == 0, 1, 3)
 
     def piece_at(i):
@@ -221,10 +219,13 @@
                 arrived(slot, p)
                 forward(slot, p, True)
                 build(slot, p)
+            if slot == 4:
+                pl.when(i + AHEAD < 8)(lambda: targets(send_kv, i + AHEAD))
+                pl.when((i + AHEAD >= 8) & (i + AHEAD < 16))(lambda: targets(send_q, i + AHEAD - 8))
 
         return carry
 
-    lax.fori_loop(0, CHIPS + 4, relay, 0)
+    lax.fori_loop(0, CHIPS + 5, relay, 0)
 
     def last(i, carry):
         for slot in (3, 1):
@@ -252,6 +253,9 @@
             return carry
 
         lax.fori_loop(0, WINDOW // PIECE, fix, 0)
+
+    scores = (even_scores, odd_scores)
+    peaks = (even_peaks, odd_peaks)
 
     def queries(i):
         p = piece_at(i)
@@ -274,7 +278,7 @@
             token = lax.broadcasted_iota(jnp.int32, s.shape, 0) % PIECE
             key = lax.broadcasted_iota(jnp.int32, s.shape, 1)
             s = jnp.where(key > token if step == 0 else key <= token, s, MASKED)
-        scores[slot, :, step * PIECE : (step + 1) * PIECE] = s
+        scores[slot][:, step * PIECE : (step + 1) * PIECE] = s
         for lane in range(0, PIECE, HEAD_DIM):
             peak = jnp.maximum(peak, s[:, lane : lane + HEAD_DIM])
         return peak
@@ -283,14 +287,14 @@
         return jnp.full((2 * PIECE, HEAD_DIM), MASKED, jnp.float32)
 
     def keep_peak(slot, peak):
-        peaks[slot] = jnp.broadcast_to(jnp.max(peak, axis=1, keepdims=True), peak.shape)
+        peaks[slot][...] = jnp.broadcast_to(jnp.max(peak, axis=1, keepdims=True), peak.shape)
 
     def mix(i, slot, step):
         p = piece_at(i)
         at = pl.ds(pl.multiple_of((p + step) * PIECE, PIECE), PIECE)
-        peak = peaks[slot]
+        peak = peaks[slot][...]
         weights = [
-            jnp.exp2(scores[slot, :, lane : lane + HEAD_DIM] - peak).astype(jnp.bfloat16)
+            jnp.exp2(scores[slot][:, lane : lane + HEAD_DIM] - peak).astype(jnp.bfloat16)
             for lane in range(step * PIECE, (step + 1) * PIECE, HEAD_DIM)
         ]
         return jnp.dot(
@@ -329,7 +333,7 @@
         peak = score(0, 0, step, peak)
     keep_peak(0, peak)
 
-    def piece(i, carry):
+    for i in range(PIECES - 1):
         slot = i % 2
         queries(i + 1)
         peak = no_peak()
@@ -340,9 +344,7 @@
             total = part if total is None else total + part
         keep_peak(1 - slot, peak)
         finish(i, total)
-        return carry
-
-    lax.fori_loop(0, PIECES - 1, piece, 0)
+
     total = None
     for step in range(STEPS):
         part = mix(PIECES - 1, (PIECES - 1) % 2, step)
@@ -372,17 +374,19 @@
     anywhere = pl.BlockSpec(memory_space=pl.ANY)
     return pl.pallas_call(
         kernel,
-        out_shape=jax.ShapeDtypeStruct(queries.shape, jnp.bfloat16),
+        out_shape=pltpu.VMEM(queries.shape, jnp.bfloat16),
         in_specs=[pl.BlockSpec(memory_space=pltpu.SMEM)] + [anywhere] * 5,
-        out_specs=anywhere,
+        out_specs=pl.BlockSpec(memory_space=pltpu.VMEM),
         scratch_shapes=[
             pltpu.VMEM((SLOTS, COLUMN, PAIR), jnp.bfloat16),
             pltpu.VMEM((COLUMN, PAIR), jnp.bfloat16),
             pltpu.VMEM((SLOTS * COLUMN, PAIR), jnp.bfloat16),
             pltpu.VMEM((SLOTS * COLUMN, PAIR), jnp.bfloat16),
             pltpu.VMEM((2 * PIECE, PAIR), jnp.bfloat16),
-            pltpu.VMEM((2, 2 * PIECE, SPAN), jnp.float32),
-            pltpu.VMEM((2, 2 * PIECE, HEAD_DIM), jnp.float32),
+            pltpu.VMEM((2 * PIECE, SPAN), jnp.float32),
+            pltpu.VMEM((2 * PIECE, SPAN), jnp.float32),
+            pltpu.VMEM((2 * PIECE, HEAD_DIM), jnp.float32),
+            pltpu.VMEM((2 * PIECE, HEAD_DIM), jnp.float32),
             pltpu.VMEM((PIECES, PIECE, PAIR), jnp.bfloat16),
             pltpu.SemaphoreType.DMA((SLOTS, CHIPS)),
             pltpu.SemaphoreType.DMA((PIECES,)),

time: 62.8 us -> 57.1 us (0.909)
  Pallas kernels: 59.2 us -> 55 us
  local copies, waits for them, and re-layouts: 1.87 us -> 0.8 us
    pallas_call x1, Pallas kernels: 59.2 us -> 55 us  [shards(): pl.pallas_call(kernel, out_shape=pltpu.VMEM(queries.shape, jnp.bfloat16),...]
    unnamed x1, local copies, waits for them, and re-layouts: 1.87 us -> 0.8 us
where the time goes in v3:
time: 57.1 us; the launch traced here: 56.4 us
  Pallas kernels  55 us (96%)
  local copies, waits for them, and re-layouts  0.8 us (1%)
  between operations  0.66 us (1%)
    pallas_call x1, Pallas kernels, shards(): pl.pallas_call(kernel, out_shape=pltpu.VMEM(queries.shape, jnp.bfloat16),...  55 us

profile of v3, /device:TPU:33, one launch (start us, length us, event | category | flops | bytes accessed | tf_op | source)
XLA Modules:
  0.0 56.4 jit_solution(440782566198418094)
XLA Ops:
  0.7 55.0 %shard_map.64 = bf16[64,4096]{1,0:T(8,128)(2,1)S(1)} custom-call(s32[1]{0:T(128)S(6)} %copy.9.start_ref, bf16[64,4096]{1,0:T(8,128)(2,1)} %q_ref.1, bf16[64,2048]{1,0:T(8,128)(2,1)} %k_ref.1, bf16[64,2048]{1,0:T(8,128)(2,1)} %v_ref.1, bf16[4096,256]{1,0:T(8,128)(2,1)} %pk_ref.1, bf16[4096,256]{1,0:T(8,128)(2,1)} %pv_ref.1), custom_call_target="tpu_custom_call" | custom-call | tf_op jit(solution)/shard_map/pallas_call | solution.py:375
  55.7 0.8 %copy.8 = bf16[64,4096]{1,0:T(8,128)(2,1)} copy(bf16[64,4096]{1,0:T(8,128)(2,1)S(1)} %shard_map.64) | data formatting | bytes 1048576

commit v4 on v3

--- a/solution.py
+++ b/solution.py
@@ -21,7 +21,7 @@
 PIECES = COLUMN // PIECE
 CHIP = 128
 CHIPS = COLUMN // CHIP
-AHEAD = 8
+AHEAD = 6
 SLOTS = 5
 SPAN = WINDOW + PIECE
 STEPS = SPAN // PIECE
@@ -221,7 +221,9 @@
                 build(slot, p)
             if slot == 4:
                 pl.when(i + AHEAD < 8)(lambda: targets(send_kv, i + AHEAD))
-                pl.when((i + AHEAD >= 8) & (i + AHEAD < 16))(lambda: targets(send_q, i + AHEAD - 8))
+                early = i + AHEAD - 8
+                for n in range(2):
+                    pl.when((early >= 0) & (early < 4))(lambda: targets(send_q, 2 * early + n))
 
         return carry
 

time: 57.1 us -> 56.5 us (0.989)
  no operation moved by 1% of the time
where the time goes in v4:
time: 56.5 us; the launch traced here: 56.4 us
  Pallas kernels  54.9 us (97%)
  local copies, waits for them, and re-layouts  0.8 us (1%)
  between operations  0.66 us (1%)
    pallas_call x1, Pallas kernels, shards(): pl.pallas_call(kernel, out_shape=pltpu.VMEM(queries.shape, jnp.bfloat16),...  54.9 us

profile of v4, /device:TPU:33, one launch (start us, length us, event | category | flops | bytes accessed | tf_op | source)
XLA Modules:
  0.0 56.4 jit_solution(10385123732757899842)
XLA Ops:
  0.7 54.9 %shard_map.64 = bf16[64,4096]{1,0:T(8,128)(2,1)S(1)} custom-call(s32[1]{0:T(128)S(6)} %copy.9.start_ref, bf16[64,4096]{1,0:T(8,128)(2,1)} %q_ref.1, bf16[64,2048]{1,0:T(8,128)(2,1)} %k_ref.1, bf16[64,2048]{1,0:T(8,128)(2,1)} %v_ref.1, bf16[4096,256]{1,0:T(8,128)(2,1)} %pk_ref.1, bf16[4096,256]{1,0:T(8,128)(2,1)} %pv_ref.1), custom_call_target="tpu_custom_call" | custom-call | tf_op jit(solution)/shard_map/pallas_call | solution.py:377
  55.6 0.8 %copy.8 = bf16[64,4096]{1,0:T(8,128)(2,1)} copy(bf16[64,4096]{1,0:T(8,128)(2,1)S(1)} %shard_map.64) | data formatting | bytes 1048576

commit v5 on v4

--- a/solution.py
+++ b/solution.py
@@ -353,7 +353,6 @@
         total = part if total is None else total + part
     finish(PIECES - 1, total)
 
-    pltpu.make_async_copy(out_ref, out_ref, o_sem).wait()
     each_target(sent)
 
     @pl.when(has_prefix)
@@ -370,6 +369,7 @@
     lax.fori_loop(0, CHIPS, forwarded, 0)
     for i in range(PIECES):
         home_copies(i, False)
+    pltpu.make_async_copy(out_ref, out_ref, o_sem).wait()
 
 
 def shards(queries, keys, values, prefix_keys, prefix_values, span_start):

time: 56.5 us -> 56.1 us (level)
  no operation moved by 1% of the time
where the time goes in v5:
time: 56.1 us; the launch traced here: 56 us
  Pallas kernels  54.5 us (97%)
  local copies, waits for them, and re-layouts  0.8 us (1%)
  between operations  0.66 us (1%)
    pallas_call x1, Pallas kernels, shards(): pl.pallas_call(kernel, out_shape=pltpu.VMEM(queries.shape, jnp.bfloat16),...  54.5 us

profile of v5, /device:TPU:33, one launch (start us, length us, event | category | flops | bytes accessed | tf_op | source)
XLA Modules:
  0.0 56.0 jit_solution(994564020875220413)
XLA Ops:
  0.7 54.5 %shard_map.64 = bf16[64,4096]{1,0:T(8,128)(2,1)S(1)} custom-call(s32[1]{0:T(128)S(6)} %copy.9.start_ref, bf16[64,4096]{1,0:T(8,128)(2,1)} %q_ref.1, bf16[64,2048]{1,0:T(8,128)(2,1)} %k_ref.1, bf16[64,2048]{1,0:T(8,128)(2,1)} %v_ref.1, bf16[4096,256]{1,0:T(8,128)(2,1)} %pk_ref.1, bf16[4096,256]{1,0:T(8,128)(2,1)} %pv_ref.1), custom_call_target="tpu_custom_call" | custom-call | tf_op jit(solution)/shard_map/pallas_call | solution.py:377
  55.2 0.8 %copy.8 = bf16[64,4096]{1,0:T(8,128)(2,1)} copy(bf16[64,4096]{1,0:T(8,128)(2,1)S(1)} %shard_map.64) | data formatting | bytes 1048576

commit v6 on v5

--- a/solution.py
+++ b/solution.py
@@ -225,15 +225,20 @@
                 for n in range(2):
                     pl.when((early >= 0) & (early < 4))(lambda: targets(send_q, 2 * early + n))
 
+        @pl.when(i >= 5)
+        def _():
+            p = (z - ring_offset(i - 5) + 8) % 8
+            arrived(1 + 2 * core, p)
+            build(1 + 2 * core, p)
+
         return carry
 
     lax.fori_loop(0, CHIPS + 5, relay, 0)
 
     def last(i, carry):
-        for slot in (3, 1):
-            p = (z - ring_offset(i) + 8) % 8
-            arrived(slot, p)
-            build(slot, p)
+        p = (z - ring_offset(i) + 8) % 8
+        arrived(3 - 2 * core, p)
+        build(3 - 2 * core, p)
         return carry
 
     lax.fori_loop(0, CHIPS, last, 0)

time: 56.1 us -> 56.1 us (level)
  no operation moved by 1% of the time
where the time goes in v6:
time: 56.1 us; the launch traced here: 56 us
  Pallas kernels  54.5 us (97%)
  local copies, waits for them, and re-layouts  0.8 us (1%)
  between operations  0.66 us (1%)
    pallas_call x1, Pallas kernels, shards(): pl.pallas_call(kernel, out_shape=pltpu.VMEM(queries.shape, jnp.bfloat16),...  54.5 us

profile of v6, /device:TPU:33, one launch (start us, length us, event | category | flops | bytes accessed | tf_op | source)
XLA Modules:
  0.0 56.0 jit_solution(3057886442300035084)
XLA Ops:
  0.7 54.5 %shard_map.64 = bf16[64,4096]{1,0:T(8,128)(2,1)S(1)} custom-call(s32[1]{0:T(128)S(6)} %copy.9.start_ref, bf16[64,4096]{1,0:T(8,128)(2,1)} %q_ref.1, bf16[64,2048]{1,0:T(8,128)(2,1)} %k_ref.1, bf16[64,2048]{1,0:T(8,128)(2,1)} %v_ref.1, bf16[4096,256]{1,0:T(8,128)(2,1)} %pk_ref.1, bf16[4096,256]{1,0:T(8,128)(2,1)} %pv_ref.1), custom_call_target="tpu_custom_call" | custom-call | tf_op jit(solution)/shard_map/pallas_call | solution.py:382
  55.2 0.8 %copy.8 = bf16[64,4096]{1,0:T(8,128)(2,1)} copy(bf16[64,4096]{1,0:T(8,128)(2,1)S(1)} %shard_map.64) | data formatting | bytes 1048576
